TPU v7x, 32 devices: a whole 2x2x4 slice. The times are simulated.
32 devices in a mesh: row: 2 (over y), col: 4 (over z), layer: 4 (over x, core).
Axes of the slice: x: 2, y: 2, z: 4, core: 2. Of those that a mesh axis runs over, the one named last changes fastest.
Arguments:
- eigvecs: float32 [16384, 8192], P('row', ('col', 'layer')), may hold values from -6 to 6
- first_vectors: float32 [16384, 128], P(('row', 'layer'), 'col'), may hold values from -0.375 to 0.375
- second_vectors: float32 [16384, 128], P(('row', 'layer'), 'col'), may hold values from -0.375 to 0.375
- first_factors: float32 [8192, 128], P(('row', 'layer'), 'col'), may hold values from -0.5 to 0.5
- second_factors: float32 [8192, 128], P(('row', 'layer'), 'col'), may hold values from -0.5 to 0.5
- panel_vectors: float32 [16384, 256], P(('row', 'layer')), may hold values from -0.125 to 0.125
- panel_factor: float32 [256, 256], replicated, may hold values from -0.375 to 0.375
Outputs:
- transformed: float32 [16384, 8192], P(('row', 'layer'), 'col')
All inputs are finite; a program needn't handle non-finite values.
Results may differ from a plain program's by a relative error of at most 0.000082.
Values sent between devices are 32-bit elements; how exact they have to be, the bound alone decides.
No kernel may reach another device: no remote copies, remote signals or barrier semaphores. Data moves between devices by JAX's collectives and lax.ppermute only.
A program may use at most 128 MiB of HBM per device.

v0:
```python
import jax
import jax.numpy as jnp
from jax import lax
from jax.sharding import PartitionSpec as P


def with_halo(array, sides, width):
    for axis, dim in sides:
        devices, length = (lax.axis_size(axis), array.shape[dim])
        up = [(i, (i + 1) % devices) for i in range(devices - 1)]
        down = [(j, i) for i, j in up]
        last = lax.slice_in_dim(array, length - width, length, axis=dim)
        first = lax.slice_in_dim(array, 0, width, axis=dim)
        before = lax.ppermute(last, axis, up)
        after = lax.ppermute(first, axis, down)
        array = jnp.concatenate([before, array, after], axis=dim)
    return array


def from_behind(value, axis, steps):
    count = lax.axis_size(axis)
    first, last = (max(0, -steps), min(count, count - steps))
    return lax.ppermute(value, axis, [(source, source + steps) for source in range(first, last)])


def apply_windows(data, vectors, factors):
    count = factors.shape[0] // 128
    width = data.shape[1]
    blocks = data.reshape(count, 256, width)
    vec_blocks = vectors.reshape(count, 256, 128)
    tri_blocks = jnp.triu(factors.reshape(count, 128, 128))
    proj = jnp.einsum("kri,krc->kic", vec_blocks, blocks, precision=lax.Precision.HIGHEST)
    scaled = jnp.einsum("kij,kjc->kic", tri_blocks, proj, precision=lax.Precision.HIGHEST)
    update = jnp.einsum("kri,kic->krc", vec_blocks, scaled, precision=lax.Precision.HIGHEST)
    return (blocks - update).reshape(count * 256, width)


def band_sweeps(data, vec_first, vec_second, fac_first, fac_second, extend, following):
    height = data.shape[0]
    width = data.shape[1]
    aligned = apply_windows(data, vec_first, fac_first)
    padded = extend(jnp.concatenate([aligned, vec_second], axis=1))
    next_factor = following(fac_second[:128])
    extended = jnp.concatenate([fac_second, next_factor], axis=0)
    offset = apply_windows(padded[:, :width], padded[:, width:], extended)
    return offset[128 : height + 128]


def band_tile(data, vec_first, vec_second, fac_first, fac_second):

    def extend(joined):
        return with_halo(joined, ((("row", "layer"), 0),), 128)

    def following(factor):
        return from_behind(factor, ("row", "layer"), -1)

    return band_sweeps(data, vec_first, vec_second, fac_first, fac_second, extend, following)


def to_tiles(data):
    return lax.all_to_all(data, "layer", split_axis=0, concat_axis=1, tiled=True)


def panel_tile(data, panel_vectors, upper):
    partial_value = jnp.dot(
        panel_vectors.T, data, precision=lax.Precision.HIGHEST, preferred_element_type=jnp.float32
    )
    projection = lax.psum(partial_value, ("row", "layer"))
    weights = jnp.dot(
        upper, projection, precision=lax.Precision.HIGHEST, preferred_element_type=jnp.float32
    )
    return data - jnp.dot(
        panel_vectors, weights, precision=lax.Precision.HIGHEST, preferred_element_type=jnp.float32
    )


def on_device(
    eigvecs,
    first_vectors,
    second_vectors,
    first_factors,
    second_factors,
    panel_vectors,
    panel_factor,
):
    upper = jnp.triu(panel_factor)
    reflectors = (
        lax.all_gather(first_vectors, "col", axis=1, tiled=True),
        lax.all_gather(second_vectors, "col", axis=1, tiled=True),
        lax.all_gather(first_factors, "col", axis=1, tiled=True),
        lax.all_gather(second_factors, "col", axis=1, tiled=True),
    )
    tiles = to_tiles(eigvecs)
    tiles = band_tile(tiles, reflectors[0], reflectors[1], reflectors[2], reflectors[3])
    return panel_tile(tiles, panel_vectors, upper)


def solution(mesh):
    in_specs = (
        P("row", ("col", "layer")),
        P(("row", "layer"), "col"),
        P(("row", "layer"), "col"),
        P(("row", "layer"), "col"),
        P(("row", "layer"), "col"),
        P(("row", "layer"), None),
        P(),
    )
    out_specs = P(("row", "layer"), "col")
    return jax.shard_map(
        on_device, mesh=mesh, in_specs=in_specs, out_specs=out_specs, check_vma=False
    )
```

profile of v0, /device:TPU:0, one launch (start us, length us, event | category | flops | bytes accessed | tf_op | source)
XLA Modules:
  0.0 561.3 jit_solution(13967101943740955004)
XLA Ops:
  6.5 7.1 %all-to-all-start = ((f32[4,2048,512]{2,1,0:T(8,128)}), f32[4,2048,512]{2,1,0:T(8,128)}, u32[]{:S(2)}, u32[]{:S(2)}) async-start(f32[4,2048,512]{2,1,0:T(8,128)} %bitcast.38), calls=%async_computation | async-start | bytes 33554432 | tf_op jit(solution)/shard_map/all_to_all | solution.py:61
  13.7 0.0 all-gather.3.cloned.1.call-start
  13.7 0.7 all-gather.3.cloned.1.call-update
  14.4 0.0 all-gather.5.cloned.1.call-start
  14.4 0.7 all-gather.5.cloned.1.call-update
  15.1 0.0 all-reduce.2.cloned.1.call-start
  15.2 0.0 copy-done.6
  15.2 20.1 %all_gather.12 = f32[1024,128]{0,1:T(8,128)S(1)} all-gather(f32[1024,32]{0,1:T(8,128)S(1)} %copy-done.6), channel_id=1, replica_groups=mesh['row'=2,'col'=4,'layer'=4] {'col'}, dimensions={1}, use_global_device_ids=true | all-gather | bytes 655360 | tf_op jit(solution)/shard_map/all_gather | solution.py:90
  35.3 1.0 copy.51
  36.4 0.1 iota_compare_fusion.2
  36.5 13.3 %all-gather.3.cloned.1.call-done = f32[2048,128]{0,1:T(8,128)} async-done(((f32[2048,32]{0,1:T(8,128)}), f32[2048,128]{0,1:T(8,128)}) %all-gather.3.cloned.1.call-update) | async-done | bytes 1048592 | tf_op jit(solution)/shard_map/all_gather | solution.py:88
  49.8 2.6 copy.41
  52.4 26.1 %all-gather.5.cloned.1.call-done = f32[2048,128]{0,1:T(8,128)} async-done(((f32[2048,32]{0,1:T(8,128)}), f32[2048,128]{0,1:T(8,128)}) %all-gather.5.cloned.1.call-update) | async-done | bytes 1048592 | tf_op jit(solution)/shard_map/all_gather | solution.py:89
  78.5 1.5 copy.43
  80.1 117.2 %all-to-all-done = f32[4,2048,512]{2,1,0:T(8,128)} async-done(((f32[4,2048,512]{2,1,0:T(8,128)}), f32[4,2048,512]{2,1,0:T(8,128)}, u32[]{:S(2)}, u32[]{:S(2)}) %all-to-all-start) | async-done | bytes 16777248 | tf_op jit(solution)/shard_map/all_to_all | solution.py:61
  197.3 20.9 %copy.39 = f32[2048,4,512]{2,1,0:T(4,128)} copy(f32[2048,4,512]{2,0,1:T(8,128)} %bitcast.1) | data formatting | bytes 33554432 | tf_op jit(solution)/shard_map/all_to_all | solution.py:61
  218.2 20.5 %reshape.28 = f32[8,256,2048]{2,1,0:T(8,128)} reshape(f32[2048,4,512]{2,1,0:T(4,128)} %copy.39) | data formatting | bytes 33554432 | tf_op jit(solution)/shard_map/reshape | solution.py:29
  238.8 14.5 %fusion.16 = f32[8,128,2048]{2,1,0:T(8,128)S(1)} fusion(f32[8,256,128]{2,1,0:T(8,128)} %bitcast.41, f32[8,256,2048]{2,1,0:T(8,128)} %reshape.28), kind=kOutput, calls=%fused_computation.29 | convolution fusion | flops 6442450944 | bytes 26214400 | tf_op jit(solution)/shard_map/kri,krc->kic/dot_general | solution.py:32
  253.3 0.0 copy-done.4
  253.3 9.6 %fusion.2 = f32[8,128,2048]{2,1,0:T(8,128)} fusion(f32[8,128,2048]{2,1,0:T(8,128)S(1)} %fusion.16, f32[8,128,128]{2,1,0:T(8,128)S(1)} %bitcast.44, pred[128,128]{1,0:T(8,128)(4,1)S(1)} %iota_compare_fusion.2), kind=kOutput, calls=%fused_computation.11 | convolution fusion | flops 3221356544 | bytes 17317888 | tf_op jit(solution)/shard_map/kij,kjc->kic/dot_general | solution.py:33
  262.9 22.4 %bitcast_subtract_fusion.1 = f32[8,256,2048]{2,1,0:T(8,128)} fusion(f32[8,256,2048]{2,1,0:T(8,128)} %reshape.28, f32[8,128,2048]{2,1,0:T(8,128)} %fusion.2, f32[8,256,128]{2,1,0:T(8,128)S(1)} %bitcast.42), kind=kOutput, calls=%fused_computation.2 | convolution fusion | flops 6446645248 | bytes 42991616 | tf_op jit(solution)/shard_map/kri,kic->krc/dot_general | solution.py:34
  285.4 3.1 pad_maximum_fusion.3
  288.5 2.3 collective-permute-start
  290.8 1.3 collective-permute-start.1
  292.1 18.3 %all_gather.15 = f32[1024,128]{0,1:T(8,128)} all-gather(f32[1024,32]{0,1:T(8,128)S(1)} %copy-done.7), channel_id=1, replica_groups=mesh['row'=2,'col'=4,'layer'=4] {'col'}, dimensions={1}, use_global_device_ids=true | all-gather | bytes 655360 | tf_op jit(solution)/shard_map/all_gather | solution.py:91
  310.3 2.0 copy.45
  312.4 0.8 slice.25
  313.2 1.3 collective-permute-start.2
  314.5 1.8 collective-permute-done.2
  316.4 1.9 pad_maximum_fusion.4
  318.3 0.0 collective-permute-done
  318.3 0.0 collective-permute-done.1
  318.3 0.0 slice-start.1
  318.3 0.0 slice-start.2
  318.3 19.1 %pad_maximum_fusion = f32[2304,2176]{1,0:T(8,128)} fusion(f32[128,2176]{1,0:T(8,128)} %collective-permute-done.1, f32[2048,128]{1,0:T(8,128)S(1)} %copy.43, f32[2048,2048]{1,0:T(8,128)} %bitcast.30, f32[128,2176]{1,0:T(8,128)} %collective-permute-done), kind=kLoop, calls=%fused_computation | loop fusion | flops 15040512 | bytes 40108032 | tf_op jit(solution)/shard_map/concatenate | solution.py:16
  337.4 15.5 %slice.24 = f32[2304,2048]{1,0:T(8,128)} slice(f32[2304,2176]{1,0:T(8,128)} %pad_maximum_fusion), slice={[0:2304], [0:2048]} | slice | bytes 37748736 | tf_op jit(solution)/shard_map/slice | solution.py:45
  352.9 1.0 pad_maximum_fusion.1
  353.9 14.0 %fusion.17 = f32[9,128,2048]{2,1,0:T(8,128)S(1)} fusion(f32[9,256,128]{2,1,0:T(8,128)S(1)} %bitcast.39, f32[9,256,2048]{2,1,0:T(8,128)} %bitcast.34), kind=kOutput, calls=%fused_computation.30 | convolution fusion | flops 7247757312 | bytes 29491200 | tf_op jit(solution)/shard_map/kri,krc->kic/dot_general | solution.py:32
  367.9 11.8 %fusion = f32[9,128,2048]{2,1,0:T(8,128)} fusion(f32[9,128,2048]{2,1,0:T(8,128)S(1)} %fusion.17, f32[9,128,128]{2,1,0:T(8,128)} %bitcast.43, pred[128,128]{1,0:T(8,128)(4,1)S(1)} %iota_compare_fusion.2), kind=kOutput, calls=%fused_computation.9 | convolution fusion | flops 3624026112 | bytes 19480576 | tf_op jit(solution)/shard_map/kij,kjc->kic/dot_general | solution.py:33
  379.7 25.0 %convolution_subtract_fusion = f32[9,256,2048]{2,1,0:T(8,128)} fusion(f32[9,256,2048]{2,1,0:T(8,128)} %bitcast.35, f32[9,256,128]{2,1,0:T(8,128)S(1)} %bitcast.40, f32[9,128,2048]{2,1,0:T(8,128)} %fusion), kind=kOutput, calls=%fused_computation.3 | convolution fusion | flops 7252475904 | bytes 48365568 | tf_op jit(solution)/shard_map/kri,kic->krc/dot_general | solution.py:34
  404.7 29.7 %convolution_bitcast_fusion = f32[256,2048]{0,1:T(8,128)} fusion(f32[2048,256]{1,0:T(8,128)S(1)} %copy-done, f32[2304,2048]{1,0:T(8,128)} %bitcast.36), kind=kOutput, calls=%fused_computation.4 | convolution fusion | flops 12884901888 | bytes 20971520 | tf_op jit(solution)/shard_map/dot_general | solution.py:65
  434.4 0.0 all-reduce.2.cloned.1.call-update
  434.5 11.8 %slice.26 = f32[2048,2048]{1,0:T(8,128)} slice(f32[2304,2048]{1,0:T(8,128)} %bitcast.37), slice={[128:2176], [0:2048]} | slice | bytes 33554432
  446.3 18.2 %copy.52 = f32[2048,2048]{0,1:T(8,128)} copy(f32[2048,2048]{1,0:T(8,128)} %slice.26) | data formatting | bytes 33554432
  464.5 35.2 %all-reduce.2.cloned.1.call-done = f32[256,2048]{0,1:T(8,128)} async-done(((f32[256,2048]{0,1:T(8,128)}), f32[256,2048]{0,1:T(8,128)}) %all-reduce.2.cloned.1.call-update) | async-done | bytes 2097168 | tf_op jit(solution)/shard_map/psum | solution.py:68
  499.7 3.5 fusion.6
  503.3 33.4 %bitcast_subtract_fusion = f32[2048,2048]{0,1:T(8,128)} fusion(f32[2048,2048]{0,1:T(8,128)} %copy.52, f32[256,2048]{1,0:T(8,128)S(1)} %fusion.6, f32[2048,256]{1,0:T(8,128)S(1)} %copy-done), kind=kOutput, calls=%fused_computation.1 | convolution fusion | flops 12889096192 | bytes 37748736 | tf_op jit(solution)/shard_map/dot_general | solution.py:72
  536.7 17.6 %copy.48 = f32[2048,2048]{1,0:T(8,128)} copy(f32[2048,2048]{0,1:T(8,128)} %bitcast_subtract_fusion) | data formatting | bytes 33554432 | tf_op jit(solution)/shard_map/sub | solution.py:72
  (23 shorter events, 0.0 us)
Async XLA Ops:
  6.5 398.2 %copy-start = (f32[2048,256]{1,0:T(8,128)S(1)}, f32[2048,256]{1,0:T(8,128)}, u32[]{:S(2)}) copy-start(f32[2048,256]{1,0:T(8,128)} %param.12) | copy-start | bytes 6291460
  6.5 8.7 %copy-start.6 = (f32[1024,32]{0,1:T(8,128)S(1)}, f32[1024,32]{0,1:T(8,128)}, u32[]{:S(2)}) copy-start(f32[1024,32]{0,1:T(8,128)} %param.10) | copy-start | bytes 393220
  6.5 190.8 %all-to-all-start = ((f32[4,2048,512]{2,1,0:T(8,128)}), f32[4,2048,512]{2,1,0:T(8,128)}, u32[]{:S(2)}, u32[]{:S(2)}) async-start(f32[4,2048,512]{2,1,0:T(8,128)} %bitcast.38), calls=%async_computation | async-start | bytes 33554432 | tf_op jit(solution)/shard_map/all_to_all | solution.py:61
  13.7 36.1 %all-gather.3.cloned.1.call-start = ((), (), s32[]{:S(2)}) async-start(), calls=%async_computation.1 | async-start | bytes 1310720 | tf_op jit(solution)/shard_map/all_gather | solution.py:88
  14.4 64.1 %all-gather.5.cloned.1.call-start = ((), (), s32[]{:S(2)}) async-start(), calls=%async_computation.2 | async-start | bytes 1310720 | tf_op jit(solution)/shard_map/all_gather | solution.py:89
  15.1 484.6 %all-reduce.2.cloned.1.call-start = ((), (), s32[]{:S(2)}) async-start(), calls=%async_computation.3 | async-start | bytes 4194304 | tf_op jit(solution)/shard_map/psum | solution.py:68
  238.8 14.5 %copy-start.4 = (f32[1024,128]{1,0:T(8,128)S(1)}, f32[1024,128]{1,0:T(8,128)}, u32[]{:S(2)}) copy-start(f32[1024,128]{1,0:T(8,128)} %copy.51) | copy-start | bytes 1572868
  253.3 9.6 %copy-start.3 = (f32[2048,128]{1,0:T(8,128)S(1)}, f32[2048,128]{1,0:T(8,128)}, u32[]{:S(2)}) copy-start(f32[2048,128]{1,0:T(8,128)} %copy.41) | copy-start | bytes 3145732
  285.4 6.7 %copy-start.7 = (f32[1024,32]{0,1:T(8,128)S(1)}, f32[1024,32]{0,1:T(8,128)}, u32[]{:S(2)}) copy-start(f32[1024,32]{0,1:T(8,128)} %param.11) | copy-start | bytes 393220
  288.5 29.8 %collective-permute-start = (f32[128,2176]{1,0:T(8,128)}, f32[128,2176]{1,0:T(8,128)}, u32[]{:S(2)}, u32[]{:S(2)}) collective-permute-start(f32[128,2176]{1,0:T(8,128)} %get-tuple-element.5), channel_id=1, source_target_pairs={{0,1},{1,2},{2,3},{3,16},{16,17},{17,18},{18,19},{4,5},{5,6},{6,7}... | collective-permute-start | bytes 3342344 | tf_op jit(solution)/shard_map/ppermute | solution.py:14
  290.8 27.5 %collective-permute-start.1 = (f32[128,2176]{1,0:T(8,128)}, f32[128,2176]{1,0:T(8,128)}, u32[]{:S(2)}, u32[]{:S(2)}) collective-permute-start(f32[128,2176]{1,0:T(8,128)} %get-tuple-element.6), channel_id=1, source_target_pairs={{1,0},{2,1},{3,2},{16,3},{17,16},{18,17},{19,18},{5,4},{6,5},{7,6}... | collective-permute-start | bytes 3342344 | tf_op jit(solution)/shard_map/ppermute | solution.py:15
  313.2 3.1 collective-permute-start.2
  318.3 34.6 %slice-start = ((s8[16777216]{0:T(1024)(128)(4,1)}), s8[4194304]{0:T(1024)(128)(4,1)S(1)}, s32[]{:S(2)}) async-start(s8[16777216]{0:T(1024)(128)(4,1)} %bitcast.31), calls=%async_computation.4 | async-start | bytes 8388608
  318.3 34.6 %slice-start.1 = ((s8[16777216]{0:T(1024)(128)(4,1)}), s8[4194304]{0:T(1024)(128)(4,1)S(1)}, s32[]{:S(2)}) async-start(s8[16777216]{0:T(1024)(128)(4,1)} %bitcast.31), calls=%async_computation.5 | async-start | bytes 8388608
  318.3 34.6 %slice-start.2 = ((s8[16777216]{0:T(1024)(128)(4,1)}), s8[4194304]{0:T(1024)(128)(4,1)S(1)}, s32[]{:S(2)}) async-start(s8[16777216]{0:T(1024)(128)(4,1)} %bitcast.31), calls=%async_computation.6 | async-start | bytes 8388608
  337.4 15.5 %slice-start.3 = ((s8[16777216]{0:T(1024)(128)(4,1)}), s8[4194304]{0:T(1024)(128)(4,1)S(1)}, s32[]{:S(2)}) async-start(s8[16777216]{0:T(1024)(128)(4,1)} %bitcast.31), calls=%async_computation.7 | async-start | bytes 8388608
  353.9 14.0 %copy-start.1 = (f32[2304,128]{1,0:T(8,128)}, f32[2304,128]{1,0:T(8,128)S(1)}, u32[]{:S(2)}) copy-start(f32[2304,128]{1,0:T(8,128)S(1)} %pad_maximum_fusion.1) | copy-start | bytes 3538948
  367.9 11.9 %copy-start.2 = (f32[2304,128]{1,0:T(8,128)S(1)}, f32[2304,128]{1,0:T(8,128)}, u32[]{:S(2)}) copy-start(f32[2304,128]{1,0:T(8,128)} %copy-done.1) | copy-start | bytes 3538948
  446.3 53.5 %copy-start.5 = (f32[256,256]{1,0:T(8,128)S(1)}, f32[256,256]{1,0:T(8,128)}, u32[]{:S(2)}) copy-start(f32[256,256]{1,0:T(8,128)} %param.13) | copy-start | bytes 786436
Sparse Core Ops, SparseCore 0:
  16.0 33.7 all-gather.2
  51.4 27.1 all-gather.4
  434.6 65.1 all-reduce.1
where the time goes:
time: 572 us; the launch traced here: 561 us
  waiting for transfers between devices  195 us (34%)
  matrix products  164 us (29%)
  local copies, waits for them, and re-layouts  113 us (20%)
  blocking collectives  38.4 us (7%)
  other arithmetic  25.2 us (4%)
  between operations  13.7 us (2%)
  starting transfers between devices  12.1 us (2%)
    all_to_all x1, waiting for transfers between devices, to_tiles(): lax.all_to_all(data, 'layer', split_axis=0, concat_axis=1, tiled=True)  117 us
    dot_general x2, matrix products, apply_windows(): jnp.einsum('kri,kic->krc', vec_blocks, scaled, precision=lax.Precision.HI...  47.4 us
    psum x1, waiting for transfers between devices, panel_tile(): projection = lax.psum(partial_value, ('row', 'layer'))  35.2 us
    dot_general x1, matrix products, panel_tile(): jnp.dot(panel_vectors, weights, precision=lax.Precision.HIGHEST, preferre...  33.4 us
    unnamed x26, local copies, waits for them, and re-layouts  30.1 us
    dot_general x1, matrix products, panel_tile(): jnp.dot(panel_vectors.T, data, precision=lax.Precision.HIGHEST, preferred...  29.7 us
    dot_general x2, matrix products, apply_windows(): jnp.einsum('kri,krc->kic', vec_blocks, blocks, precision=lax.Precision.HI...  28.5 us
    all_gather x1, waiting for transfers between devices, on_device(): lax.all_gather(second_vectors, 'col', axis=1, tiled=True)  26.1 us
  transfers between devices with their start and end apart: 7, of which 5 were waited for; matrix products, arithmetic and copies ran while one was open for 7% of the time, Pallas kernels for 0%

commit v1 on v0

--- a/solution.py
+++ b/solution.py
@@ -1,7 +1,17 @@
+import functools
 import jax
 import jax.numpy as jnp
 from jax import lax
 from jax.sharding import PartitionSpec as P
+
+
+def meet_shards(piece_in, peer_axis, net_axis):
+    for m in (peer_axis, net_axis):
+        piece_in = lax.psum(piece_in, m)
+    return piece_in
+
+
+enter_grid = functools.partial(meet_shards, peer_axis="layer", net_axis="row")
 
 
 def with_halo(array, sides, width):
@@ -65,7 +75,7 @@
     partial_value = jnp.dot(
         panel_vectors.T, data, precision=lax.Precision.HIGHEST, preferred_element_type=jnp.float32
     )
-    projection = lax.psum(partial_value, ("row", "layer"))
+    projection = enter_grid(partial_value)
     weights = jnp.dot(
         upper, projection, precision=lax.Precision.HIGHEST, preferred_element_type=jnp.float32
     )

time: 572 us -> 627 us (1.096)
  waiting for transfers between devices: 195 us -> 250 us
    psum x1 -> x2, waiting for transfers between devices: 35.2 us -> 90 us  [meet_shards(): piece_in = lax.psum(piece_in, m)]
  transfers between devices with their start and end apart: 7 -> 8, of which waited for: 5 -> 6; matrix products, arithmetic and copies ran while one was open for 7% -> 7% of each run, Pallas kernels for 0% -> 0%
where the time goes in v1:
time: 627 us; the launch traced here: 616 us
  waiting for transfers between devices  250 us (40%)
  matrix products  164 us (26%)
  local copies, waits for them, and re-layouts  113 us (18%)
  blocking collectives  38.4 us (6%)
  other arithmetic  25.2 us (4%)
  between operations  13.8 us (2%)
  starting transfers between devices  12.1 us (2%)
    all_to_all x1, waiting for transfers between devices, to_tiles(): lax.all_to_all(data, 'layer', split_axis=0, concat_axis=1, tiled=True)  117 us
    psum x2, waiting for transfers between devices, meet_shards(): piece_in = lax.psum(piece_in, m)  90 us
    dot_general x2, matrix products, apply_windows(): jnp.einsum('kri,kic->krc', vec_blocks, scaled, precision=lax.Precision.HI...  47.4 us
    dot_general x1, matrix products, panel_tile(): jnp.dot(panel_vectors, weights, precision=lax.Precision.HIGHEST, preferre...  33.4 us
    unnamed x26, local copies, waits for them, and re-layouts  30.1 us
    dot_general x1, matrix products, panel_tile(): jnp.dot(panel_vectors.T, data, precision=lax.Precision.HIGHEST, preferred...  29.7 us
    dot_general x2, matrix products, apply_windows(): jnp.einsum('kri,krc->kic', vec_blocks, blocks, precision=lax.Precision.HI...  28.5 us
    all_gather x1, waiting for transfers between devices, on_device(): lax.all_gather(second_vectors, 'col', axis=1, tiled=True)  26.1 us
  transfers between devices with their start and end apart: 8, of which 6 were waited for; matrix products, arithmetic and copies ran while one was open for 7% of the time, Pallas kernels for 0%

profile of v1, /device:TPU:0, one launch (start us, length us, event | category | flops | bytes accessed | tf_op | source)
XLA Modules:
  0.0 616.1 jit_solution(15783956645319989436)
XLA Ops:
  6.5 7.1 %all-to-all-start = ((f32[4,2048,512]{2,1,0:T(8,128)}), f32[4,2048,512]{2,1,0:T(8,128)}, u32[]{:S(2)}, u32[]{:S(2)}) async-start(f32[4,2048,512]{2,1,0:T(8,128)} %bitcast.38), calls=%async_computation | async-start | bytes 33554432 | tf_op jit(solution)/shard_map/all_to_all | solution.py:71
  13.7 0.0 all-gather.3.cloned.1.call-start
  13.7 0.7 all-gather.3.cloned.1.call-update
  14.4 0.0 all-gather.5.cloned.1.call-start
  14.4 0.7 all-gather.5.cloned.1.call-update
  15.1 0.0 all-reduce.3.cloned.1.call-start
  15.2 20.1 %all_gather.12 = f32[1024,128]{0,1:T(8,128)S(1)} all-gather(f32[1024,32]{0,1:T(8,128)S(1)} %copy-done.6), channel_id=1, replica_groups=mesh['row'=2,'col'=4,'layer'=4] {'col'}, dimensions={1}, use_global_device_ids=true | all-gather | bytes 655360 | tf_op jit(solution)/shard_map/all_gather | solution.py:100
  35.3 1.0 copy.51
  36.4 0.1 iota_compare_fusion.2
  36.5 13.3 %all-gather.3.cloned.1.call-done = f32[2048,128]{0,1:T(8,128)} async-done(((f32[2048,32]{0,1:T(8,128)}), f32[2048,128]{0,1:T(8,128)}) %all-gather.3.cloned.1.call-update) | async-done | bytes 1048592 | tf_op jit(solution)/shard_map/all_gather | solution.py:98
  49.8 2.6 copy.41
  52.4 26.1 %all-gather.5.cloned.1.call-done = f32[2048,128]{0,1:T(8,128)} async-done(((f32[2048,32]{0,1:T(8,128)}), f32[2048,128]{0,1:T(8,128)}) %all-gather.5.cloned.1.call-update) | async-done | bytes 1048592 | tf_op jit(solution)/shard_map/all_gather | solution.py:99
  78.5 1.5 copy.43
  80.1 117.2 %all-to-all-done = f32[4,2048,512]{2,1,0:T(8,128)} async-done(((f32[4,2048,512]{2,1,0:T(8,128)}), f32[4,2048,512]{2,1,0:T(8,128)}, u32[]{:S(2)}, u32[]{:S(2)}) %all-to-all-start) | async-done | bytes 16777248 | tf_op jit(solution)/shard_map/all_to_all | solution.py:71
  197.3 20.9 %copy.39 = f32[2048,4,512]{2,1,0:T(4,128)} copy(f32[2048,4,512]{2,0,1:T(8,128)} %bitcast.1) | data formatting | bytes 33554432 | tf_op jit(solution)/shard_map/all_to_all | solution.py:71
  218.2 20.5 %reshape.28 = f32[8,256,2048]{2,1,0:T(8,128)} reshape(f32[2048,4,512]{2,1,0:T(4,128)} %copy.39) | data formatting | bytes 33554432 | tf_op jit(solution)/shard_map/reshape | solution.py:39
  238.8 14.5 %fusion.16 = f32[8,128,2048]{2,1,0:T(8,128)S(1)} fusion(f32[8,256,128]{2,1,0:T(8,128)} %bitcast.41, f32[8,256,2048]{2,1,0:T(8,128)} %reshape.28), kind=kOutput, calls=%fused_computation.29 | convolution fusion | flops 6442450944 | bytes 26214400 | tf_op jit(solution)/shard_map/kri,krc->kic/dot_general | solution.py:42
  253.3 9.6 %fusion.2 = f32[8,128,2048]{2,1,0:T(8,128)} fusion(f32[8,128,2048]{2,1,0:T(8,128)S(1)} %fusion.16, f32[8,128,128]{2,1,0:T(8,128)S(1)} %bitcast.44, pred[128,128]{1,0:T(8,128)(4,1)S(1)} %iota_compare_fusion.2), kind=kOutput, calls=%fused_computation.11 | convolution fusion | flops 3221356544 | bytes 17317888 | tf_op jit(solution)/shard_map/kij,kjc->kic/dot_general | solution.py:43
  262.9 22.4 %bitcast_subtract_fusion.1 = f32[8,256,2048]{2,1,0:T(8,128)} fusion(f32[8,256,2048]{2,1,0:T(8,128)} %reshape.28, f32[8,128,2048]{2,1,0:T(8,128)} %fusion.2, f32[8,256,128]{2,1,0:T(8,128)S(1)} %bitcast.42), kind=kOutput, calls=%fused_computation.2 | convolution fusion | flops 6446645248 | bytes 42991616 | tf_op jit(solution)/shard_map/kri,kic->krc/dot_general | solution.py:44
  285.4 3.1 pad_maximum_fusion.3
  288.5 2.3 collective-permute-start
  290.8 1.3 collective-permute-start.1
  292.1 18.3 %all_gather.15 = f32[1024,128]{0,1:T(8,128)} all-gather(f32[1024,32]{0,1:T(8,128)S(1)} %copy-done.7), channel_id=1, replica_groups=mesh['row'=2,'col'=4,'layer'=4] {'col'}, dimensions={1}, use_global_device_ids=true | all-gather | bytes 655360 | tf_op jit(solution)/shard_map/all_gather | solution.py:101
  310.3 2.0 copy.45
  312.4 0.8 slice.25
  313.2 1.3 collective-permute-start.2
  314.5 1.8 collective-permute-done.2
  316.4 1.9 pad_maximum_fusion.4
  318.3 0.0 collective-permute-done
  318.3 0.0 collective-permute-done.1
  318.3 0.0 slice-start.1
  318.3 19.1 %pad_maximum_fusion = f32[2304,2176]{1,0:T(8,128)} fusion(f32[128,2176]{1,0:T(8,128)} %collective-permute-done.1, f32[2048,128]{1,0:T(8,128)S(1)} %copy.43, f32[2048,2048]{1,0:T(8,128)} %bitcast.30, f32[128,2176]{1,0:T(8,128)} %collective-permute-done), kind=kLoop, calls=%fused_computation | loop fusion | flops 15040512 | bytes 40108032 | tf_op jit(solution)/shard_map/concatenate | solution.py:26
  337.4 15.5 %slice.24 = f32[2304,2048]{1,0:T(8,128)} slice(f32[2304,2176]{1,0:T(8,128)} %pad_maximum_fusion), slice={[0:2304], [0:2048]} | slice | bytes 37748736 | tf_op jit(solution)/shard_map/slice | solution.py:55
  352.9 1.0 pad_maximum_fusion.1
  353.9 14.0 %fusion.17 = f32[9,128,2048]{2,1,0:T(8,128)S(1)} fusion(f32[9,256,128]{2,1,0:T(8,128)S(1)} %bitcast.39, f32[9,256,2048]{2,1,0:T(8,128)} %bitcast.34), kind=kOutput, calls=%fused_computation.30 | convolution fusion | flops 7247757312 | bytes 29491200 | tf_op jit(solution)/shard_map/kri,krc->kic/dot_general | solution.py:42
  367.9 11.8 %fusion = f32[9,128,2048]{2,1,0:T(8,128)} fusion(f32[9,128,2048]{2,1,0:T(8,128)S(1)} %fusion.17, f32[9,128,128]{2,1,0:T(8,128)} %bitcast.43, pred[128,128]{1,0:T(8,128)(4,1)S(1)} %iota_compare_fusion.2), kind=kOutput, calls=%fused_computation.9 | convolution fusion | flops 3624026112 | bytes 19480576 | tf_op jit(solution)/shard_map/kij,kjc->kic/dot_general | solution.py:43
  379.7 25.0 %convolution_subtract_fusion = f32[9,256,2048]{2,1,0:T(8,128)} fusion(f32[9,256,2048]{2,1,0:T(8,128)} %bitcast.35, f32[9,256,128]{2,1,0:T(8,128)S(1)} %bitcast.40, f32[9,128,2048]{2,1,0:T(8,128)} %fusion), kind=kOutput, calls=%fused_computation.3 | convolution fusion | flops 7252475904 | bytes 48365568 | tf_op jit(solution)/shard_map/kri,kic->krc/dot_general | solution.py:44
  404.7 29.7 %convolution_bitcast_fusion = f32[256,2048]{0,1:T(8,128)} fusion(f32[2048,256]{1,0:T(8,128)S(1)} %copy-done, f32[2304,2048]{1,0:T(8,128)} %bitcast.36), kind=kOutput, calls=%fused_computation.4 | convolution fusion | flops 12884901888 | bytes 20971520 | tf_op jit(solution)/shard_map/dot_general | solution.py:75
  434.4 0.0 all-reduce.3.cloned.1.call-update
  434.4 0.0 all-reduce.5.cloned.1.call-start
  434.5 54.8 %all-reduce.3.cloned.1.call-done = f32[256,2048]{0,1:T(8,128)} async-done(((f32[256,2048]{0,1:T(8,128)}), f32[256,2048]{0,1:T(8,128)}) %all-reduce.3.cloned.1.call-update) | async-done | bytes 2097168 | tf_op jit(solution)/shard_map/psum | solution.py:10
  489.3 0.0 all-reduce.5.cloned.1.call-update
  489.4 12.2 %slice.26 = f32[2048,2048]{1,0:T(8,128)} slice(f32[2304,2048]{1,0:T(8,128)} %bitcast.37), slice={[128:2176], [0:2048]} | slice | bytes 33554432
  501.6 17.8 %copy.52 = f32[2048,2048]{0,1:T(8,128)} copy(f32[2048,2048]{1,0:T(8,128)} %slice.26) | data formatting | bytes 33554432
  519.4 35.1 %all-reduce.5.cloned.1.call-done = f32[256,2048]{0,1:T(8,128)} async-done(((f32[256,2048]{0,1:T(8,128)}), f32[256,2048]{0,1:T(8,128)}) %all-reduce.5.cloned.1.call-update) | async-done | bytes 2097168 | tf_op jit(solution)/shard_map/psum | solution.py:10
  554.6 3.5 fusion.6
  558.1 33.4 %bitcast_subtract_fusion = f32[2048,2048]{0,1:T(8,128)} fusion(f32[2048,2048]{0,1:T(8,128)} %copy.52, f32[256,2048]{1,0:T(8,128)S(1)} %fusion.6, f32[2048,256]{1,0:T(8,128)S(1)} %copy-done), kind=kOutput, calls=%fused_computation.1 | convolution fusion | flops 12889096192 | bytes 37748736 | tf_op jit(solution)/shard_map/dot_general | solution.py:82
  591.5 17.6 %copy.48 = f32[2048,2048]{1,0:T(8,128)} copy(f32[2048,2048]{0,1:T(8,128)} %bitcast_subtract_fusion) | data formatting | bytes 33554432 | tf_op jit(solution)/shard_map/sub | solution.py:82
  (26 shorter events, 0.1 us)
Async XLA Ops:
  6.5 398.2 %copy-start = (f32[2048,256]{1,0:T(8,128)S(1)}, f32[2048,256]{1,0:T(8,128)}, u32[]{:S(2)}) copy-start(f32[2048,256]{1,0:T(8,128)} %param.12) | copy-start | bytes 6291460
  6.5 8.7 %copy-start.6 = (f32[1024,32]{0,1:T(8,128)S(1)}, f32[1024,32]{0,1:T(8,128)}, u32[]{:S(2)}) copy-start(f32[1024,32]{0,1:T(8,128)} %param.10) | copy-start | bytes 393220
  6.5 190.8 %all-to-all-start = ((f32[4,2048,512]{2,1,0:T(8,128)}), f32[4,2048,512]{2,1,0:T(8,128)}, u32[]{:S(2)}, u32[]{:S(2)}) async-start(f32[4,2048,512]{2,1,0:T(8,128)} %bitcast.38), calls=%async_computation | async-start | bytes 33554432 | tf_op jit(solution)/shard_map/all_to_all | solution.py:71
  13.7 36.1 %all-gather.3.cloned.1.call-start = ((), (), s32[]{:S(2)}) async-start(), calls=%async_computation.1 | async-start | bytes 1310720 | tf_op jit(solution)/shard_map/all_gather | solution.py:98
  14.4 64.1 %all-gather.5.cloned.1.call-start = ((), (), s32[]{:S(2)}) async-start(), calls=%async_computation.2 | async-start | bytes 1310720 | tf_op jit(solution)/shard_map/all_gather | solution.py:99
  15.1 474.2 %all-reduce.3.cloned.1.call-start = ((), (), s32[]{:S(2)}) async-start(), calls=%async_computation.3 | async-start | bytes 4194304 | tf_op jit(solution)/shard_map/psum | solution.py:10
  238.8 14.5 %copy-start.4 = (f32[1024,128]{1,0:T(8,128)S(1)}, f32[1024,128]{1,0:T(8,128)}, u32[]{:S(2)}) copy-start(f32[1024,128]{1,0:T(8,128)} %copy.51) | copy-start | bytes 1572868
  253.3 9.6 %copy-start.3 = (f32[2048,128]{1,0:T(8,128)S(1)}, f32[2048,128]{1,0:T(8,128)}, u32[]{:S(2)}) copy-start(f32[2048,128]{1,0:T(8,128)} %copy.41) | copy-start | bytes 3145732
  285.4 6.7 %copy-start.7 = (f32[1024,32]{0,1:T(8,128)S(1)}, f32[1024,32]{0,1:T(8,128)}, u32[]{:S(2)}) copy-start(f32[1024,32]{0,1:T(8,128)} %param.11) | copy-start | bytes 393220
  288.5 29.8 %collective-permute-start = (f32[128,2176]{1,0:T(8,128)}, f32[128,2176]{1,0:T(8,128)}, u32[]{:S(2)}, u32[]{:S(2)}) collective-permute-start(f32[128,2176]{1,0:T(8,128)} %get-tuple-element.5), channel_id=1, source_target_pairs={{0,1},{1,2},{2,3},{3,16},{16,17},{17,18},{18,19},{4,5},{5,6},{6,7}... | collective-permute-start | bytes 3342344 | tf_op jit(solution)/shard_map/ppermute | solution.py:24
  290.8 27.5 %collective-permute-start.1 = (f32[128,2176]{1,0:T(8,128)}, f32[128,2176]{1,0:T(8,128)}, u32[]{:S(2)}, u32[]{:S(2)}) collective-permute-start(f32[128,2176]{1,0:T(8,128)} %get-tuple-element.6), channel_id=1, source_target_pairs={{1,0},{2,1},{3,2},{16,3},{17,16},{18,17},{19,18},{5,4},{6,5},{7,6}... | collective-permute-start | bytes 3342344 | tf_op jit(solution)/shard_map/ppermute | solution.py:25
  313.2 3.1 collective-permute-start.2
  318.3 34.6 %slice-start = ((s8[16777216]{0:T(1024)(128)(4,1)}), s8[4194304]{0:T(1024)(128)(4,1)S(1)}, s32[]{:S(2)}) async-start(s8[16777216]{0:T(1024)(128)(4,1)} %bitcast.31), calls=%async_computation.5 | async-start | bytes 8388608
  318.3 34.6 %slice-start.1 = ((s8[16777216]{0:T(1024)(128)(4,1)}), s8[4194304]{0:T(1024)(128)(4,1)S(1)}, s32[]{:S(2)}) async-start(s8[16777216]{0:T(1024)(128)(4,1)} %bitcast.31), calls=%async_computation.6 | async-start | bytes 8388608
  318.3 34.6 %slice-start.2 = ((s8[16777216]{0:T(1024)(128)(4,1)}), s8[4194304]{0:T(1024)(128)(4,1)S(1)}, s32[]{:S(2)}) async-start(s8[16777216]{0:T(1024)(128)(4,1)} %bitcast.31), calls=%async_computation.7 | async-start | bytes 8388608
  337.4 15.5 %slice-start.3 = ((s8[16777216]{0:T(1024)(128)(4,1)}), s8[4194304]{0:T(1024)(128)(4,1)S(1)}, s32[]{:S(2)}) async-start(s8[16777216]{0:T(1024)(128)(4,1)} %bitcast.31), calls=%async_computation.8 | async-start | bytes 8388608
  353.9 14.0 %copy-start.1 = (f32[2304,128]{1,0:T(8,128)}, f32[2304,128]{1,0:T(8,128)S(1)}, u32[]{:S(2)}) copy-start(f32[2304,128]{1,0:T(8,128)S(1)} %pad_maximum_fusion.1) | copy-start | bytes 3538948
  367.9 11.9 %copy-start.2 = (f32[2304,128]{1,0:T(8,128)S(1)}, f32[2304,128]{1,0:T(8,128)}, u32[]{:S(2)}) copy-start(f32[2304,128]{1,0:T(8,128)} %copy-done.1) | copy-start | bytes 3538948
  434.4 120.1 %all-reduce.5.cloned.1.call-start = ((), (), s32[]{:S(2)}) async-start(), calls=%async_computation.4 | async-start | bytes 4194304 | tf_op jit(solution)/shard_map/psum | solution.py:10
  501.6 52.9 %copy-start.5 = (f32[256,256]{1,0:T(8,128)S(1)}, f32[256,256]{1,0:T(8,128)}, u32[]{:S(2)}) copy-start(f32[256,256]{1,0:T(8,128)} %param.13) | copy-start | bytes 786436
Sparse Core Ops, SparseCore 0:
  16.0 33.7 all-gather.2
  51.4 27.1 all-gather.4
  434.6 54.7 all-reduce.2
  491.5 63.0 all-reduce.4
